TPU v7x, 32 devices: a whole 2x2x4 slice. The times are simulated.
32 devices in a mesh: ctx: 32 (over z, y, x, core).
Axes of the slice: x: 2, y: 2, z: 4, core: 2. Of those that a mesh axis runs over, the one named last changes fastest.
Arguments:
- queries: bfloat16 [32768, 2048], P('ctx'), may hold values from -6 to 6
- keys: bfloat16 [32768, 2048], P('ctx'), may hold values from -6 to 6
- values: bfloat16 [32768, 2048], P('ctx'), may hold values from -6 to 6
- level_gate: bfloat16 [32768, 128], P('ctx'), may hold values from 0.19921875 to 2
- norm_gain: float32 [2048], replicated, may hold values from 0.5 to 1.5
- out_weight: bfloat16 [2048, 2048], P('ctx'), may hold values from -0.125 to 0.125
Outputs:
- layer_out: bfloat16 [32768, 2048], P('ctx')
All inputs are finite; a program needn't handle non-finite values.
Results may differ from a plain program's by a relative error of at most 0.0057.
Values may be sent and summed in bfloat16 or wider, within the bound.
A program may use at most 192 MiB of HBM per device.

v0:
```python
import jax
import jax.numpy as jnp
from jax import lax
from jax.sharding import PartitionSpec as P

HEADS = 16
HEAD = 128
GATES = 8


EPSILON = 1e-06


def from_partner(value, axis, bit):
    mask = 2**bit
    pairs = [(source, source ^ mask) for source in range(lax.axis_size(axis))]
    return lax.ppermute(value, axis, pairs)


def shards(queries, keys, values, level_gate, norm_gain, out_weight):
    rows_here = queries.shape[0]
    query_heads = queries.reshape(rows_here, HEADS, HEAD)
    key_heads = keys.reshape(rows_here, HEADS, HEAD)
    value_heads = values.reshape(rows_here, HEADS, HEAD)
    level_weights = level_gate.reshape(rows_here, GATES, HEADS).astype(jnp.float32)
    scores = jnp.einsum("thd,shd->hts", query_heads, key_heads, preferred_element_type=jnp.float32)
    positions = jnp.arange(rows_here, dtype=jnp.int32)
    causal = positions[:, None] >= positions[None, :]
    weighted = jnp.where(causal[None], scores, jnp.float32(0.0)).astype(jnp.bfloat16)
    summed = jnp.einsum("hts,shd->thd", weighted, value_heads, preferred_element_type=jnp.float32)
    summed = summed * level_weights[:, 0, :, None]
    own_state = jnp.einsum(
        "shd,she->hde", key_heads, value_heads, preferred_element_type=jnp.float32
    )
    position = lax.axis_index("ctx")
    levels = lax.axis_size("ctx").bit_length() - 1
    running = own_state
    for level_index in range(levels):
        partner = from_partner(running, "ctx", level_index)
        upper_half = position >> level_index & 1 == 1
        bucket = jnp.where(upper_half, partner, jnp.float32(0.0)).astype(jnp.bfloat16)
        product = jnp.einsum(
            "thd,hde->the", query_heads, bucket, preferred_element_type=jnp.float32
        )
        summed = summed + level_weights[:, level_index + 1, :, None] * product
        if level_index + 1 < levels:
            running = running + partner
    squares = jnp.mean(summed * summed, axis=-1, keepdims=True)
    normed = summed * lax.rsqrt(squares + EPSILON) * norm_gain.reshape(HEADS, HEAD)
    normed = normed.reshape(rows_here, HEADS * HEAD).astype(jnp.bfloat16)
    whole_weight = lax.all_gather(out_weight, "ctx", axis=0, tiled=True)
    projected = jnp.dot(normed, whole_weight, preferred_element_type=jnp.float32)
    return projected.astype(jnp.bfloat16)


def solution(mesh):
    placed = (P("ctx", None), P("ctx", None), P("ctx", None), P("ctx", None), P(), P("ctx", None))
    return jax.shard_map(
        shards, mesh=mesh, in_specs=placed, out_specs=P("ctx", None), check_vma=False
    )
```

profile of v0, /device:TPU:0, one launch (start us, length us, event | category | flops | bytes accessed | tf_op | source)
XLA Modules:
  0.0 195.6 jit_solution(12585109822985198153)
XLA Ops:
  7.3 6.4 %copy.45 = bf16[1024,2048]{0,1:T(8,128)(2,1)} copy(bf16[1024,2048]{1,0:T(8,128)(2,1)} %param.7) | data formatting | bytes 8388608 | tf_op jit(solution)/shard_map/reshape | solution.py:23
  13.7 4.8 %fusion.11 = f32[16,128,128]{2,1,0:T(8,128)S(1)} fusion(bf16[1024,16,128]{0,2,1:T(8,128)(2,1)} %bitcast.103, bf16[1024,2048]{1,0:T(8,128)(2,1)} %param.8), kind=kOutput, calls=%fused_computation.19 | convolution fusion | flops 536870912 | bytes 9437184 | tf_op jit(solution)/shard_map/shd,she->hde/dot_general | solution.py:32
  19.1 2.3 %collective-permute-done = f32[16,128,128]{2,1,0:T(8,128)S(1)} collective-permute-done((f32[16,128,128]{2,1,0:T(8,128)S(1)}, f32[16,128,128]{2,1,0:T(8,128)S(1)}, u32[]{:S(2)}, u32[]{:S(2)}) %collective-permute-start) | collective-permute-done | bytes 1048608 | tf_op jit(solution)/shard_map/ppermute | solution.py:17
  21.5 2.9 %collective-permute-start.1 = (f32[16,128,128]{2,1,0:T(8,128)S(1)}, f32[16,128,128]{2,1,0:T(8,128)S(1)}, u32[]{:S(2)}, u32[]{:S(2)}) collective-permute-start(f32[16,128,128]{2,1,0:T(8,128)S(1)} %add.39), channel_id=1, source_target_pairs={{0,2},{1,3},{2,0},{3,1},{4,6},{5,7},{6,4},{7,5},{8,10},{9,11},{10,... | collective-permute-start | bytes 3145736 | tf_op jit(solution)/shard_map/ppermute | solution.py:17
  24.4 1.3 iota_compare_fusion
  25.6 30.2 %collective-permute-done.1 = f32[16,128,128]{2,1,0:T(8,128)S(1)} collective-permute-done((f32[16,128,128]{2,1,0:T(8,128)S(1)}, f32[16,128,128]{2,1,0:T(8,128)S(1)}, u32[]{:S(2)}, u32[]{:S(2)}) %collective-permute-start.1) | collective-permute-done | bytes 1048608 | tf_op jit(solution)/shard_map/ppermute | solution.py:17
  56.0 1.7 collective-permute-start.2
  57.7 23.8 %fusion = f32[16,1024,128]{1,2,0:T(8,128)} fusion(pred[1024,1024]{1,0:T(8,128)(4,1)} %iota_compare_fusion, bf16[1024,16,128]{0,2,1:T(8,128)(2,1)} %bitcast.104, bf16[1024,2048]{1,0:T(8,128)(2,1)} %param.8, bf16[1024,2048]{1,0:T(8,128)(2,1)} %param.6), kind=kOutput, calls=%fused_computation.1 | convolution fusion | flops 8623489024 | bytes 22020096 | tf_op jit(solution)/shard_map/hts,shd->thd/dot_general | solution.py:30
  81.5 1.1 copy.27
  82.6 0.8 convert.1
  83.4 1.0 slice_bitcast_fusion.5
  84.5 7.0 %fusion.23 = f32[16,128,1024]{2,1,0:T(8,128)} fusion(f32[16,128,128]{2,1,0:T(8,128)S(1)} %collective-permute-done, pred[]{:T(512)S(6)} %eq.15, bf16[1024,2048]{1,0:T(8,128)(2,1)} %param.6), kind=kOutput, calls=%fused_computation.30 | convolution fusion | flops 537133056 | bytes 13631489 | tf_op jit(solution)/shard_map/thd,hde->the/dot_general | solution.py:42
  91.5 1.8 collective-permute-done.2
  93.3 1.3 add.43
  94.6 1.2 collective-permute-start.3
  95.8 4.6 %fusion.19 = f32[16,128,1024]{2,1,0:T(8,128)} fusion(f32[16,128,128]{2,1,0:T(8,128)S(1)} %collective-permute-done.1, pred[]{:T(512)S(6)} %eq.16, bf16[1024,2048]{1,0:T(8,128)(2,1)S(1)} %copy-done), kind=kOutput, calls=%fused_computation.27 | convolution fusion | flops 537133056 | bytes 13631489 | tf_op jit(solution)/shard_map/thd,hde->the/dot_general | solution.py:42
  100.4 4.6 %fusion.17 = f32[16,128,1024]{2,1,0:T(8,128)} fusion(f32[16,128,128]{2,1,0:T(8,128)} %collective-permute-done.2, pred[]{:T(512)S(6)} %eq.17, bf16[1024,2048]{1,0:T(8,128)(2,1)S(1)} %copy-done), kind=kOutput, calls=%fused_computation.25 | convolution fusion | flops 537133056 | bytes 13631489 | tf_op jit(solution)/shard_map/thd,hde->the/dot_general | solution.py:42
  105.0 20.6 %collective-permute-done.3 = f32[16,128,128]{2,1,0:T(8,128)S(1)} collective-permute-done((f32[16,128,128]{2,1,0:T(8,128)S(1)}, f32[16,128,128]{2,1,0:T(8,128)S(1)}, u32[]{:S(2)}, u32[]{:S(2)}) %collective-permute-start.3) | collective-permute-done | bytes 1048608 | tf_op jit(solution)/shard_map/ppermute | solution.py:17
  125.8 1.9 collective-permute-start.4
  127.6 4.6 %fusion.15 = f32[16,128,1024]{2,1,0:T(8,128)} fusion(f32[16,128,128]{2,1,0:T(8,128)S(1)} %collective-permute-done.3, pred[]{:T(512)S(6)} %eq.18, bf16[1024,2048]{1,0:T(8,128)(2,1)S(1)} %copy-done), kind=kOutput, calls=%fused_computation.23 | convolution fusion | flops 537133056 | bytes 13631489 | tf_op jit(solution)/shard_map/thd,hde->the/dot_general | solution.py:42
  132.2 17.3 %collective-permute-done.4 = bf16[16,128,128]{2,1,0:T(8,128)(2,1)S(1)} collective-permute-done((bf16[16,128,128]{2,1,0:T(8,128)(2,1)S(1)}, bf16[16,128,128]{2,1,0:T(8,128)(2,1)S(1)}, u32[]{:S(2)}, u32[]{:S(2)}) %collective-permute-start.4) | collective-permute-done | bytes 524320 | tf_op jit(solution)/shard_map/ppermute | solution.py:17
  149.6 19.9 %multiply_reduce_fusion = (f32[1024,16]{0,1:T(8,128)S(1)}, f32[1024,16,128]{0,2,1:T(8,128)}) fusion(bf16[16,128,128]{2,1,0:T(8,128)(2,1)S(1)} %collective-permute-done.4, pred[]{:T(512)S(6)} %eq.19, f32[1024,16]{0,1:T(8,128)S(1)} %get-tuple-element.6, f32[16,128,1024]{2,1,0:T(8,128)} %fusion.15, f32[1024,16]{0,1:T(8,128)S(1)} %get-tuple-element.7, ...), kind=kOutput, calls=%fused_computation.17 | convolution fusion | flops 564379648 | bytes 55508992 | tf_op jit(solution)/shard_map/thd,hde->the/dot_general | solution.py:42
  169.5 5.3 %multiply_convert_fusion = bf16[1024,16,128]{0,2,1:T(8,128)(2,1)} fusion(f32[1024,16,128]{0,2,1:T(8,128)} %get-tuple-element.12, f32[16,128]{1,0:T(8,128)S(1)} %bitcast.107, f32[1024,16]{0,1:T(8,128)S(1)} %add_rsqrt_fusion), kind=kLoop, calls=%fused_computation.16 | loop fusion | flops 6291456 | bytes 12656640 | tf_op jit(solution)/shard_map/convert_element_type | solution.py:50
  174.8 14.0 %convolution_convert_fusion = bf16[1024,2048]{1,0:T(8,128)(2,1)} fusion(bf16[1024,2048]{0,1:T(8,128)(2,1)} %bitcast.105, bf16[2048,2048]{1,0:T(8,128)(2,1)} %all-gather.2.cloned.1.call-done), kind=kOutput, calls=%fused_computation.33 | convolution fusion | flops 8592031744 | bytes 16777216 | tf_op jit(solution)/shard_map/dot_general | solution.py:52
  (12 shorter events, 1.7 us)
Async XLA Ops:
  6.5 168.3 %all-gather.2.cloned.1.call-start = ((), (), s32[]{:S(2)}) async-start(), calls=%async_computation | async-start | bytes 8650752 | tf_op jit(solution)/shard_map/all_gather | solution.py:51
  18.5 2.8 %collective-permute-start = (f32[16,128,128]{2,1,0:T(8,128)S(1)}, f32[16,128,128]{2,1,0:T(8,128)S(1)}, u32[]{:S(2)}, u32[]{:S(2)}) collective-permute-start(f32[16,128,128]{2,1,0:T(8,128)S(1)} %fusion.11), channel_id=1, source_target_pairs={{0,1},{1,0},{2,3},{3,2},{4,5},{5,4},{6,7},{7,6},{8,9},{9,8},{10,11... | collective-permute-start | bytes 3145736 | tf_op jit(solution)/shard_map/ppermute | solution.py:17
  21.5 34.4 %collective-permute-start.1 = (f32[16,128,128]{2,1,0:T(8,128)S(1)}, f32[16,128,128]{2,1,0:T(8,128)S(1)}, u32[]{:S(2)}, u32[]{:S(2)}) collective-permute-start(f32[16,128,128]{2,1,0:T(8,128)S(1)} %add.39), channel_id=1, source_target_pairs={{0,2},{1,3},{2,0},{3,1},{4,6},{5,7},{6,4},{7,5},{8,10},{9,11},{10,... | collective-permute-start | bytes 3145736 | tf_op jit(solution)/shard_map/ppermute | solution.py:17
  56.0 37.2 %collective-permute-start.2 = (f32[16,128,128]{2,1,0:T(8,128)S(1)}, f32[16,128,128]{2,1,0:T(8,128)}, u32[]{:S(2)}, u32[]{:S(2)}) collective-permute-start(f32[16,128,128]{2,1,0:T(8,128)S(1)} %add.41), channel_id=1, source_target_pairs={{0,4},{1,5},{2,6},{3,7},{4,0},{5,1},{6,2},{7,3},{8,12},{9,13},{10,... | collective-permute-start | bytes 3145736 | tf_op jit(solution)/shard_map/ppermute | solution.py:17
  84.5 11.3 %copy-start = (bf16[1024,2048]{1,0:T(8,128)(2,1)S(1)}, bf16[1024,2048]{1,0:T(8,128)(2,1)}, u32[]{:S(2)}) copy-start(bf16[1024,2048]{1,0:T(8,128)(2,1)} %param.6) | copy-start | bytes 12582916
  94.6 31.0 %collective-permute-start.3 = (f32[16,128,128]{2,1,0:T(8,128)S(1)}, f32[16,128,128]{2,1,0:T(8,128)S(1)}, u32[]{:S(2)}, u32[]{:S(2)}) collective-permute-start(f32[16,128,128]{2,1,0:T(8,128)S(1)} %add.43), channel_id=1, source_target_pairs={{0,8},{1,9},{2,10},{3,11},{4,12},{5,13},{6,14},{7,15},{8,0},{9,1},... | collective-permute-start | bytes 3145736 | tf_op jit(solution)/shard_map/ppermute | solution.py:17
  125.8 23.8 %collective-permute-start.4 = (bf16[16,128,128]{2,1,0:T(8,128)(2,1)S(1)}, bf16[16,128,128]{2,1,0:T(8,128)(2,1)S(1)}, u32[]{:S(2)}, u32[]{:S(2)}) collective-permute-start(bf16[16,128,128]{2,1,0:T(8,128)(2,1)S(1)} %add.45), channel_id=1, source_target_pairs={{0,16},{1,17},{2,18},{3,19},{4,20},{5,21},{6,22},{7,23},{8,24},{9,... | collective-permute-start | bytes 1572872 | tf_op jit(solution)/shard_map/ppermute | solution.py:17
  149.6 19.9 %copy-start.1 = (f32[2048]{0:T(1024)S(1)}, f32[2048]{0:T(1024)}, u32[]{:S(2)}) copy-start(f32[2048]{0:T(1024)} %param.10) | copy-start | bytes 24580
Sparse Core Ops, SparseCore 0:
  10.2 101.7 all-gather.1
where the time goes:
time: 196 us
  matrix products  83.4 us (43%)
  waiting for transfers between devices  72.9 us (37%)
  between operations  13.5 us (7%)
  other arithmetic  9.13 us (5%)
  local copies, waits for them, and re-layouts  8.52 us (4%)
  starting transfers between devices  8.22 us (4%)
    ppermute x5, waiting for transfers between devices, from_partner(): return lax.ppermute(value, axis, pairs)  72.2 us
    dot_general x5, matrix products, shards(): jnp.einsum('thd,hde->the', query_heads, bucket, preferred_element_type=jn...  40.7 us
    dot_general x1, matrix products, shards(): jnp.einsum('hts,shd->thd', weighted, value_heads, preferred_element_type=...  23.8 us
    dot_general x1, matrix products, shards(): jnp.dot(normed, whole_weight, preferred_element_type=jnp.float32)  14 us
    ppermute x5, starting transfers between devices, from_partner(): return lax.ppermute(value, axis, pairs)  8.21 us
    reshape x1, local copies, waits for them, and re-layouts, shards(): key_heads = keys.reshape(rows_here, HEADS, HEAD)  6.4 us
    convert_element_type x1, other arithmetic, shards(): normed = normed.reshape(rows_here, HEADS * HEAD).astype(jnp.bfloat16)  5.29 us
    dot_general x1, matrix products, shards(): jnp.einsum('shd,she->hde', key_heads, value_heads, preferred_element_type...  4.83 us
  transfers between devices with their start and end apart: 6, of which 5 were waited for; matrix products, arithmetic and copies ran while one was open for 44% of the time, Pallas kernels for 0%

commit v1 on v0

v1 whole, which is shorter than its diff:
```python
import functools
import jax
import jax.numpy as jnp
from jax import lax
from jax.experimental import pallas as pl
from jax.experimental.pallas import tpu as pltpu
from jax.sharding import PartitionSpec as P

HEAD = 128
CHUNK = 256
EPSILON = 1e-06
F32 = jnp.float32
BF16 = jnp.bfloat16


def dot(a, b, dims):
    return lax.dot_general(a, b, (dims, ((), ())), preferred_element_type=F32)


def states_kernel(heads, chunks, k_ref, v_ref, prefix_ref, total_ref):
    for h in range(heads):
        cols = slice(h * HEAD, (h + 1) * HEAD)
        running = None
        for c in range(chunks):
            rows = slice(c * CHUNK, (c + 1) * CHUNK)
            one = dot(k_ref[rows, cols], v_ref[rows, cols], ((0,), (0,)))
            prefix_ref[c, h] = (jnp.zeros_like(one) if running is None else running).astype(BF16)
            running = one if running is None else running + one
        total_ref[h] = running


def chunk_states(keys, values):
    rows, width = keys.shape
    heads, chunks = width // HEAD, rows // CHUNK
    per = 4
    while heads % per:
        per //= 2
    return pl.pallas_call(
        functools.partial(states_kernel, per, chunks),
        grid=(heads // per,),
        in_specs=[pl.BlockSpec((rows, per * HEAD), lambda i: (0, i))] * 2,
        out_specs=[
            pl.BlockSpec((chunks, per, HEAD, HEAD), lambda i: (0, i, 0, 0)),
            pl.BlockSpec((per, HEAD, HEAD), lambda i: (i, 0, 0)),
        ],
        out_shape=[
            jax.ShapeDtypeStruct((chunks, heads, HEAD, HEAD), BF16),
            jax.ShapeDtypeStruct((heads, HEAD, HEAD), F32),
        ],
        cost_estimate=pl.CostEstimate(flops=2 * rows * width * HEAD, bytes_accessed=4 * rows * width, transcendentals=0),
        name="states",
    )(keys, values)


def local_kernel(heads, q_ref, k_ref, v_ref, gate_ref, prefix_ref, out_ref):
    gate = gate_ref[...].astype(F32)
    rows = lax.broadcasted_iota(jnp.int32, (CHUNK, CHUNK), 0)
    cols = lax.broadcasted_iota(jnp.int32, (CHUNK, CHUNK), 1)
    causal = rows >= cols
    for h in range(heads):
        at = slice(h * HEAD, (h + 1) * HEAD)
        q = q_ref[:, at]
        scores = dot(q, k_ref[:, at], ((1,), (1,)))
        scores = jnp.where(causal, scores, 0.0).astype(BF16)
        mixed = dot(scores, v_ref[:, at], ((1,), (0,))) + dot(q, prefix_ref[0, h], ((1,), (0,)))
        out_ref[:, at] = mixed * gate[:, h : h + 1]


def local_term(queries, keys, values, gate, prefix):
    rows, width = queries.shape
    heads, chunks = width // HEAD, rows // CHUNK
    row_block = pl.BlockSpec((CHUNK, width), lambda i: (i, 0))
    return pl.pallas_call(
        functools.partial(local_kernel, heads),
        grid=(chunks,),
        in_specs=[
            row_block,
            row_block,
            row_block,
            pl.BlockSpec((CHUNK, gate.shape[1]), lambda i: (i, 0)),
            pl.BlockSpec((1, heads, HEAD, HEAD), lambda i: (i, 0, 0, 0)),
        ],
        out_specs=row_block,
        out_shape=jax.ShapeDtypeStruct((rows, width), F32),
        cost_estimate=pl.CostEstimate(flops=10 * rows * width * CHUNK, bytes_accessed=10 * rows * width, transcendentals=0),
        name="local",
    )(queries, keys, values, gate, prefix)


def finish_kernel(heads, levels, q_ref, local_ref, gate_ref, gain_ref, bucket_ref, w_ref, out_ref, normed_ref):
    gate = gate_ref[...].astype(F32)
    for h in range(heads):
        at = slice(h * HEAD, (h + 1) * HEAD)
        product = dot(q_ref[:, at], bucket_ref[h], ((1,), (0,)))
        total = local_ref[:, at]
        for level in range(levels):
            lane = (level + 1) * heads + h
            total = total + gate[:, lane : lane + 1] * product[:, level * HEAD : (level + 1) * HEAD]
        squares = jnp.mean(total * total, axis=-1, keepdims=True)
        normed = total * lax.rsqrt(squares + EPSILON) * gain_ref[:, at]
        normed_ref[:, at] = normed.astype(BF16)
    out_ref[...] = jnp.dot(normed_ref[...], w_ref[...], preferred_element_type=F32).astype(BF16)


def finish(queries, local, gate, gain, buckets, weight):
    rows, width = queries.shape
    heads = width // HEAD
    levels = buckets.shape[2] // HEAD
    out_width = weight.shape[1]
    row_block = pl.BlockSpec((CHUNK, width), lambda i: (i, 0))
    once = pl.Buffered(1)
    return pl.pallas_call(
        functools.partial(finish_kernel, heads, levels),
        grid=(rows // CHUNK,),
        in_specs=[
            row_block,
            row_block,
            pl.BlockSpec((CHUNK, gate.shape[1]), lambda i: (i, 0)),
            pl.BlockSpec((1, width), lambda i: (0, 0)),
            pl.BlockSpec(buckets.shape, lambda i: (0, 0, 0), pipeline_mode=once),
            pl.BlockSpec(weight.shape, lambda i: (0, 0), pipeline_mode=once),
        ],
        out_specs=pl.BlockSpec((CHUNK, out_width), lambda i: (i, 0)),
        out_shape=jax.ShapeDtypeStruct((rows, out_width), BF16),
        scratch_shapes=[pltpu.VMEM((CHUNK, width), BF16)],
        cost_estimate=pl.CostEstimate(flops=4 * rows * width * out_width, bytes_accessed=20 * rows * width, transcendentals=0),
        name="finish",
    )(queries, local, gate, gain, buckets, weight)


def exchange(value, axis, bit):
    pairs = [(source, source ^ 2**bit) for source in range(lax.axis_size(axis))]
    return lax.ppermute(value, axis, pairs)


def shards(queries, keys, values, level_gate, norm_gain, out_weight):
    heads = queries.shape[1] // HEAD
    half = heads // 2
    position = lax.axis_index("ctx")
    levels = lax.axis_size("ctx").bit_length() - 1
    whole_weight = lax.all_gather(out_weight, "ctx", axis=0, tiled=True)
    prefix, total = chunk_states(keys, values)
    odd = position & 1 == 1
    from_pair = exchange(total.astype(BF16), "ctx", 0)
    first = jnp.where(odd, from_pair, jnp.zeros_like(from_pair))
    both = total + from_pair.astype(F32)
    running = jnp.where(odd, both[half:], both[:half])
    mine = []
    for level in range(1, levels):
        partner = exchange(running.astype(BF16), "ctx", level)
        upper = position >> level & 1 == 1
        mine.append(jnp.where(upper, partner, jnp.zeros_like(partner)))
        running = running + partner.astype(F32)
    mine = jnp.stack(mine, 0)
    other = exchange(mine, "ctx", 0)
    low = jnp.where(odd, other, mine)
    high = jnp.where(odd, mine, other)
    rest = jnp.concatenate([low, high], 1)
    buckets = jnp.concatenate([first[None], rest], 0)
    buckets = buckets.transpose(1, 2, 0, 3).reshape(heads, HEAD, levels * HEAD)
    local = local_term(queries, keys, values, level_gate, prefix)
    return finish(queries, local, level_gate, norm_gain.reshape(1, -1), buckets, whole_weight)


def solution(mesh):
    placed = (P("ctx", None), P("ctx", None), P("ctx", None), P("ctx", None), P(), P("ctx", None))
    return jax.shard_map(
        shards, mesh=mesh, in_specs=placed, out_specs=P("ctx", None), check_vma=False
    )
```

time: 196 us -> 139 us (0.71)
  matrix products: 83.4 us -> 0 us
  Pallas kernels: 0 us -> 51.6 us
  waiting for transfers between devices: 72.9 us -> 52.2 us
  other arithmetic: 9.13 us -> 4.73 us
    dot_general x8 -> x0, matrix products: 83.4 us -> none  [the longest x5 40.7 us: shards(): jnp.einsum('thd,hde->the', query_heads, bucket, preferred_element_type=jn...]
    pallas_call x0 -> x3, Pallas kernels: none -> 51.6 us  [the longest x1 32.7 us: finish(): pl.pallas_call(functools.partial(finish_kernel, heads, levels), grid=(row...]
    ppermute x5 -> x6, waiting for transfers between devices: 72.2 us -> 40.3 us  [exchange(): return lax.ppermute(value, axis, pairs)]
    all_gather x1, waiting for transfers between devices: 0.01 us -> 11.2 us  [shards(): whole_weight = lax.all_gather(out_weight, 'ctx', axis=0, tiled=True)]
    convert_element_type x2 -> x5, other arithmetic: 6.14 us -> 1.67 us  [the longest x1 1.31 us: shards(): from_pair = exchange(total.astype(BF16), 'ctx', 0)]
    transpose x0 -> x1, local copies, waits for them, and re-layouts: none -> 2.56 us  [shards(): buckets = buckets.transpose(1, 2, 0, 3).reshape(heads, HEAD, levels * HEAD)]
    reshape x1, local copies, waits for them, and re-layouts: 6.4 us -> 4.42 us  [shards(): buckets = buckets.transpose(1, 2, 0, 3).reshape(heads, HEAD, levels * HEAD)]
    ppermute x5 -> x6, starting transfers between devices: 8.21 us -> 9.43 us  [exchange(): return lax.ppermute(value, axis, pairs)]
  transfers between devices with their start and end apart: 6 -> 7, of which waited for: 5 -> 6; matrix products, arithmetic and copies ran while one was open for 44% -> 8% of each run, Pallas kernels for 0% -> 14%
where the time goes in v1:
time: 139 us; the launch traced here: 138 us
  waiting for transfers between devices  52.2 us (38%)
  Pallas kernels  51.6 us (37%)
  between operations  13.5 us (10%)
  starting transfers between devices  9.43 us (7%)
  local copies, waits for them, and re-layouts  6.98 us (5%)
  other arithmetic  4.73 us (3%)
    ppermute x6, waiting for transfers between devices, exchange(): return lax.ppermute(value, axis, pairs)  40.3 us
    pallas_call x1, Pallas kernels, finish(): pl.pallas_call(functools.partial(finish_kernel, heads, levels), grid=(row...  32.7 us
    pallas_call x1, Pallas kernels, local_term(): pl.pallas_call(functools.partial(local_kernel, heads), grid=(chunks,), in...  12.6 us
    all_gather x1, waiting for transfers between devices, shards(): whole_weight = lax.all_gather(out_weight, 'ctx', axis=0, tiled=True)  11.2 us
    ppermute x6, starting transfers between devices, exchange(): return lax.ppermute(value, axis, pairs)  9.43 us
    pallas_call x1, Pallas kernels, chunk_states(): pl.pallas_call(functools.partial(states_kernel, per, chunks), grid=(heads...  6.29 us
    reshape x1, local copies, waits for them, and re-layouts, shards(): buckets = buckets.transpose(1, 2, 0, 3).reshape(heads, HEAD, levels * HEAD)  4.42 us
  transfers between devices with their start and end apart: 7, of which 6 were waited for; matrix products, arithmetic and copies ran while one was open for 8% of the time, Pallas kernels for 14%

profile of v1, /device:TPU:0, one launch (start us, length us, event | category | flops | bytes accessed | tf_op | source)
XLA Modules:
  0.0 138.4 jit_solution(4121201489108625306)
XLA Ops:
  6.5 0.7 all-gather.2.cloned.1.call-update
  7.3 6.3 %states.1 = (bf16[4,16,128,128]{3,2,1,0:T(8,128)(2,1)}, f32[16,128,128]{2,1,0:T(8,128)}) custom-call(bf16[1024,2048]{1,0:T(8,128)(2,1)} %k_ref.3, bf16[1024,2048]{1,0:T(8,128)(2,1)} %v_ref.3), custom_call_target="tpu_custom_call" | custom-call | flops 536870912 | bytes 8388608 | tf_op jit(solution)/shard_map/states/pallas_call | solution.py:38
  13.5 1.3 convert_element_type.27
  14.9 0.6 collective-permute-start
  15.4 1.5 %collective-permute-done = bf16[16,128,128]{2,1,0:T(8,128)(2,1)S(1)} collective-permute-done((bf16[16,128,128]{2,1,0:T(8,128)(2,1)S(1)}, bf16[16,128,128]{2,1,0:T(8,128)(2,1)S(1)}, u32[]{:S(2)}, u32[]{:S(2)}) %collective-permute-start) | collective-permute-done | bytes 524320 | tf_op jit(solution)/shard_map/ppermute | solution.py:133
  17.0 1.3 convert_add_fusion
  18.4 2.9 %collective-permute-start.1 = (bf16[8,128,128]{2,1,0:T(8,128)(2,1)S(1)}, bf16[8,128,128]{2,1,0:T(8,128)(2,1)S(1)}, u32[]{:S(2)}, u32[]{:S(2)}) collective-permute-start(bf16[8,128,128]{2,1,0:T(8,128)(2,1)S(1)} %get-tuple-element.9), channel_id=1, source_target_pairs={{0,2},{1,3},{2,0},{3,1},{4,6},{5,7},{6,4},{7,5},{8,10},{9,11},{10,... | collective-permute-start | bytes 786440 | tf_op jit(solution)/shard_map/ppermute | solution.py:133
  21.3 8.5 %collective-permute-done.1 = bf16[8,128,128]{2,1,0:T(8,128)(2,1)S(1)} collective-permute-done((bf16[8,128,128]{2,1,0:T(8,128)(2,1)S(1)}, bf16[8,128,128]{2,1,0:T(8,128)(2,1)S(1)}, u32[]{:S(2)}, u32[]{:S(2)}) %collective-permute-start.1) | collective-permute-done | bytes 262176 | tf_op jit(solution)/shard_map/ppermute | solution.py:133
  29.8 1.8 %collective-permute-start.2 = (bf16[8,128,128]{2,1,0:T(8,128)(2,1)S(1)}, bf16[8,128,128]{2,1,0:T(8,128)(2,1)S(1)}, u32[]{:S(2)}, u32[]{:S(2)}) collective-permute-start(bf16[8,128,128]{2,1,0:T(8,128)(2,1)S(1)} %fusion), channel_id=1, source_target_pairs={{0,4},{1,5},{2,6},{3,7},{4,0},{5,1},{6,2},{7,3},{8,12},{9,13},{10,... | collective-permute-start | bytes 786440 | tf_op jit(solution)/shard_map/ppermute | solution.py:133
  31.7 6.0 %collective-permute-done.2 = bf16[8,128,128]{2,1,0:T(8,128)(2,1)S(1)} collective-permute-done((bf16[8,128,128]{2,1,0:T(8,128)(2,1)S(1)}, bf16[8,128,128]{2,1,0:T(8,128)(2,1)S(1)}, u32[]{:S(2)}, u32[]{:S(2)}) %collective-permute-start.2) | collective-permute-done | bytes 262176 | tf_op jit(solution)/shard_map/ppermute | solution.py:133
  37.7 0.1 fusion.1
  37.8 1.7 %collective-permute-start.3 = (bf16[8,128,128]{2,1,0:T(8,128)(2,1)S(1)}, bf16[8,128,128]{2,1,0:T(8,128)(2,1)S(1)}, u32[]{:S(2)}, u32[]{:S(2)}) collective-permute-start(bf16[8,128,128]{2,1,0:T(8,128)(2,1)S(1)} %fusion.1), channel_id=1, source_target_pairs={{0,8},{1,9},{2,10},{3,11},{4,12},{5,13},{6,14},{7,15},{8,0},{9,1},... | collective-permute-start | bytes 786440 | tf_op jit(solution)/shard_map/ppermute | solution.py:133
  39.5 14.5 %collective-permute-done.3 = bf16[8,128,128]{2,1,0:T(8,128)(2,1)S(1)} collective-permute-done((bf16[8,128,128]{2,1,0:T(8,128)(2,1)S(1)}, bf16[8,128,128]{2,1,0:T(8,128)(2,1)S(1)}, u32[]{:S(2)}, u32[]{:S(2)}) %collective-permute-start.3) | collective-permute-done | bytes 262176 | tf_op jit(solution)/shard_map/ppermute | solution.py:133
  54.0 0.1 add_convert_fusion
  54.2 2.4 %collective-permute-start.4 = (bf16[8,128,128]{2,1,0:T(8,128)(2,1)S(1)}, bf16[8,128,128]{2,1,0:T(8,128)(2,1)S(1)}, u32[]{:S(2)}, u32[]{:S(2)}) collective-permute-start(bf16[8,128,128]{2,1,0:T(8,128)(2,1)S(1)} %add_convert_fusion), channel_id=1, source_target_pairs={{0,16},{1,17},{2,18},{3,19},{4,20},{5,21},{6,22},{7,23},{8,24},{9,... | collective-permute-start | bytes 786440 | tf_op jit(solution)/shard_map/ppermute | solution.py:133
  56.6 9.7 %collective-permute-done.4 = bf16[8,128,128]{2,1,0:T(8,128)(2,1)S(1)} collective-permute-done((bf16[8,128,128]{2,1,0:T(8,128)(2,1)S(1)}, bf16[8,128,128]{2,1,0:T(8,128)(2,1)S(1)}, u32[]{:S(2)}, u32[]{:S(2)}) %collective-permute-start.4) | collective-permute-done | bytes 262176 | tf_op jit(solution)/shard_map/ppermute | solution.py:133
  66.4 1.1 pad_maximum_fusion
  67.5 12.6 %local.1.local_ref = f32[1024,2048]{1,0:T(8,128)} custom-call(bf16[1024,2048]{1,0:T(8,128)(2,1)} %q_ref.3, bf16[1024,2048]{1,0:T(8,128)(2,1)} %k_ref.3, bf16[1024,2048]{1,0:T(8,128)(2,1)} %v_ref.3, bf16[1024,128]{1,0:T(8,128)(2,1)} %gate_ref.3, bf16[4,16,128,128]{3,2,1,0:T(8,128)(2,1)} %get-tuple-element.7.prefix_ref), custom_call_target="tpu_custom_call" | custom-call | flops 5368709120 | bytes 20971520 | tf_op jit(solution)/shard_map/local/pallas_call | solution.py:73
  80.2 0.2 broadcast_select_fusion.1
  80.3 0.3 maximum_bitcast_fusion
  80.7 2.6 %copy.8 = bf16[16,128,5,128]{1,3,2,0:T(8,128)(2,1)} copy(bf16[16,128,5,128]{3,1,0,2:T(8,128)(2,1)S(1)} %maximum_bitcast_fusion) | data formatting | bytes 5242880 | tf_op jit(solution)/shard_map/transpose | solution.py:160
  83.2 4.4 %copy.9.bucket_ref = bf16[16,128,640]{2,1,0:T(8,128)(2,1)} copy(bf16[16,128,640]{1,2,0:T(8,128)(2,1)} %bitcast.14) | data formatting | bytes 5242880 | tf_op jit(solution)/shard_map/reshape | solution.py:160
  87.6 11.2 %all-gather.2.cloned.1.call-done.w_ref = bf16[2048,2048]{1,0:T(8,128)(2,1)} async-done(((bf16[64,2048]{1,0:T(8,128)(2,1)}), bf16[2048,2048]{1,0:T(8,128)(2,1)}) %all-gather.2.cloned.1.call-update) | async-done | bytes 8388624 | tf_op jit(solution)/shard_map/all_gather | solution.py:141
  98.8 32.7 %finish.1 = bf16[1024,2048]{1,0:T(8,128)(2,1)} custom-call(bf16[1024,2048]{1,0:T(8,128)(2,1)} %q_ref.3, f32[1024,2048]{1,0:T(8,128)} %local.1.local_ref, bf16[1024,128]{1,0:T(8,128)(2,1)} %gate_ref.3, f32[1,2048]{1,0:T(1,128)} %bitcast.15, bf16[16,128,640]{2,1,0:T(8,128)(2,1)} %copy.9.bucket_ref, bf16[2048,2048]{1,0:T(8,128)(2,1)} %all-gather.2.cloned.1.call-done.w_ref), custom_call_target="tpu_custom_call" | custom-call | flops 17179869184 | bytes 41943040 | tf_op jit(solution)/shard_map/finish/pallas_call | solution.py:112
  (10 shorter events, 0.3 us)
Async XLA Ops:
  6.5 92.3 %all-gather.2.cloned.1.call-start = ((), (), s32[]{:S(2)}) async-start(), calls=%async_computation | async-start | bytes 8650752 | tf_op jit(solution)/shard_map/all_gather | solution.py:141
  14.9 2.1 %collective-permute-start = (bf16[16,128,128]{2,1,0:T(8,128)(2,1)S(1)}, bf16[16,128,128]{2,1,0:T(8,128)(2,1)S(1)}, u32[]{:S(2)}, u32[]{:S(2)}) collective-permute-start(bf16[16,128,128]{2,1,0:T(8,128)(2,1)S(1)} %convert_element_type.27), channel_id=1, source_target_pairs={{0,1},{1,0},{2,3},{3,2},{4,5},{5,4},{6,7},{7,6},{8,9},{9,8},{10,11... | collective-permute-start | bytes 1572872 | tf_op jit(solution)/shard_map/ppermute | solution.py:133
  18.4 11.4 %collective-permute-start.1 = (bf16[8,128,128]{2,1,0:T(8,128)(2,1)S(1)}, bf16[8,128,128]{2,1,0:T(8,128)(2,1)S(1)}, u32[]{:S(2)}, u32[]{:S(2)}) collective-permute-start(bf16[8,128,128]{2,1,0:T(8,128)(2,1)S(1)} %get-tuple-element.9), channel_id=1, source_target_pairs={{0,2},{1,3},{2,0},{3,1},{4,6},{5,7},{6,4},{7,5},{8,10},{9,11},{10,... | collective-permute-start | bytes 786440 | tf_op jit(solution)/shard_map/ppermute | solution.py:133
  29.8 7.8 %collective-permute-start.2 = (bf16[8,128,128]{2,1,0:T(8,128)(2,1)S(1)}, bf16[8,128,128]{2,1,0:T(8,128)(2,1)S(1)}, u32[]{:S(2)}, u32[]{:S(2)}) collective-permute-start(bf16[8,128,128]{2,1,0:T(8,128)(2,1)S(1)} %fusion), channel_id=1, source_target_pairs={{0,4},{1,5},{2,6},{3,7},{4,0},{5,1},{6,2},{7,3},{8,12},{9,13},{10,... | collective-permute-start | bytes 786440 | tf_op jit(solution)/shard_map/ppermute | solution.py:133
  37.8 16.2 %collective-permute-start.3 = (bf16[8,128,128]{2,1,0:T(8,128)(2,1)S(1)}, bf16[8,128,128]{2,1,0:T(8,128)(2,1)S(1)}, u32[]{:S(2)}, u32[]{:S(2)}) collective-permute-start(bf16[8,128,128]{2,1,0:T(8,128)(2,1)S(1)} %fusion.1), channel_id=1, source_target_pairs={{0,8},{1,9},{2,10},{3,11},{4,12},{5,13},{6,14},{7,15},{8,0},{9,1},... | collective-permute-start | bytes 786440 | tf_op jit(solution)/shard_map/ppermute | solution.py:133
  54.2 12.2 %collective-permute-start.4 = (bf16[8,128,128]{2,1,0:T(8,128)(2,1)S(1)}, bf16[8,128,128]{2,1,0:T(8,128)(2,1)S(1)}, u32[]{:S(2)}, u32[]{:S(2)}) collective-permute-start(bf16[8,128,128]{2,1,0:T(8,128)(2,1)S(1)} %add_convert_fusion), channel_id=1, source_target_pairs={{0,16},{1,17},{2,18},{3,19},{4,20},{5,21},{6,22},{7,23},{8,24},{9,... | collective-permute-start | bytes 786440 | tf_op jit(solution)/shard_map/ppermute | solution.py:133
  67.5 12.7 %collective-permute-start.5 = (bf16[4,8,128,128]{3,2,1,0:T(8,128)(2,1)}, bf16[4,8,128,128]{3,2,1,0:T(8,128)(2,1)S(1)}, u32[]{:S(2)}, u32[]{:S(2)}) collective-permute-start(bf16[4,8,128,128]{3,2,1,0:T(8,128)(2,1)} %pad_maximum_fusion), channel_id=1, source_target_pairs={{0,1},{1,0},{2,3},{3,2},{4,5},{5,4},{6,7},{7,6},{8,9},{9,8},{10,11... | collective-permute-start | bytes 3145736 | tf_op jit(solution)/shard_map/ppermute | solution.py:133
Sparse Core Ops, SparseCore 0:
  10.2 88.6 all-gather.1

commit v2 on v0

v2 whole, which is shorter than its diff:
```python
import functools
import jax
import jax.numpy as jnp
from jax import lax
from jax.experimental import pallas as pl
from jax.experimental.pallas import tpu as pltpu
from jax.sharding import PartitionSpec as P

HEAD = 128
CHUNK = 256
EPSILON = 1e-06
F32 = jnp.float32
BF16 = jnp.bfloat16
MESH = pl.DeviceIdType.MESH


def dot(a, b, dims):
    return lax.dot_general(a, b, (dims, ((), ())), preferred_element_type=F32)


def other(me, mask):
    bit = 1
    out = me
    while bit <= mask:
        if mask & bit:
            out = out + bit * (1 - 2 * ((me // bit) % 2))
        bit *= 2
    return out


def transfers(levels, columns):
    names = [("stage", l) for l in range(levels)] + [("pass", l) for l in range(1, levels)]
    names += [("z", j) for j in range(1, columns)]
    for kind in ("x", "y", "dx", "dy", "c0", "c2", "c4", "c6"):
        names += [(kind, j) for j in range(columns)]
    return {name: at for at, name in enumerate(names)}


def kernel(n, q_hbm, k_hbm, v_hbm, gate_ref, gain_ref, w_ref, out_hbm,
           q, k, v, whole, acc, prefix, total, running, buckets, first, sends, load_sem, send_sem, recv_sem):
    rows, width = q.shape
    heads, chunks = width // HEAD, rows // CHUNK
    half = heads // 2
    levels = n.bit_length() - 1
    columns = n // 8
    part = w_ref.shape[0]
    ids = transfers(levels, columns)
    me = lax.axis_index("ctx")
    core = me % 2
    mine = pl.ds(core * half, half)
    yours = pl.ds((1 - core) * half, half)

    def load(hbm, buffer, kind, c):
        at = pl.ds(c * CHUNK, CHUNK)
        return pltpu.make_async_copy(hbm.at[at], buffer.at[at], load_sem.at[kind, c])

    for c in range(chunks):
        load(k_hbm, k, 0, c).start()
        load(v_hbm, v, 1, c).start()
    for c in range(chunks):
        load(q_hbm, q, 2, c).start()

    masks = sorted({1 << l for l in range(levels)} | {j << 3 for j in range(1, columns)})
    barrier = pltpu.get_barrier_semaphore()
    for mask in masks:
        pl.semaphore_signal(barrier, inc=1, device_id=(other(me, mask),), device_id_type=MESH)
    pl.semaphore_wait(barrier, len(masks))

    def copy(name, src, dst, mask):
        at = ids[name]
        return pltpu.make_async_remote_copy(
            src_ref=src, dst_ref=dst, send_sem=send_sem.at[at], recv_sem=recv_sem.at[at],
            device_id=(other(me, mask),), device_id_type=MESH,
        )

    def shard(mask, side=None):
        at = pl.ds(pl.multiple_of(other(me, mask) * part, part), part)
        if side is None:
            return whole.at[at]
        width_here = whole.shape[1] // 2
        return whole.at[at, pl.ds(side * width_here, width_here)]

    def send(name):
        kind, j = name
        if kind == "stage":
            if j == 0:
                return copy(name, first, buckets.at[0], 1)
            return copy(name, sends.at[j - 1], buckets.at[j, mine], 1 << j)
        if kind == "pass":
            return copy(name, buckets.at[j, mine], buckets.at[j, mine], 1)
        col = j << 3
        if kind == "z":
            return copy(name, w_ref, shard(0), col)
        if kind in ("x", "y", "c0"):
            mask = {"x": 2, "y": 4, "c0": 1}[kind]
            return copy(name, w_ref if j == 0 else shard(col), shard(col), mask)
        if kind == "dy":
            return copy(name, shard(2 ^ col, 0), shard(2 ^ col, 0), 4)
        if kind == "dx":
            return copy(name, shard(4 ^ col, 1), shard(4 ^ col, 1), 2)
        group = int(kind[1])
        return copy(name, shard(group ^ col), shard(group ^ col), 1)

    def arrival(name):
        kind, j = name
        if kind == "stage":
            dst, mask = (buckets.at[0], 1) if j == 0 else (buckets.at[j, mine], 1 << j)
        elif kind == "pass":
            dst, mask = buckets.at[j, yours], 1
        else:
            col = j << 3
            if kind == "z":
                dst, mask = shard(col), col
            elif kind in ("x", "y"):
                mask = {"x": 2, "y": 4}[kind]
                dst = shard(mask ^ col)
            elif kind == "dy":
                dst, mask = shard(6 ^ col, 0), 4
            elif kind == "dx":
                dst, mask = shard(6 ^ col, 1), 2
            else:
                dst, mask = shard(1 ^ int(kind[1]) ^ col), 1
        return copy(name, dst, dst, mask)

    def start(*name):
        send(name).start()

    def receive(*name):
        arrival(name).wait_recv()

    own = pltpu.make_async_copy(w_ref, shard(0), load_sem.at[3, 0])
    own.start()
    for j in range(1, columns):
        start("z", j)
    start("x", 0)
    start("y", 0)
    start("c0", 0)

    total[...] = jnp.zeros_like(total)

    def state_step(c, carry):
        load(k_hbm, k, 0, c).wait()
        load(v_hbm, v, 1, c).wait()
        at = pl.ds(pl.multiple_of(c * CHUNK, CHUNK), CHUNK)
        for h in range(heads):
            cols = slice(h * HEAD, (h + 1) * HEAD)
            before = total[h]
            prefix[c, h] = before.astype(BF16)
            total[h] = before + dot(k[at, cols], v[at, cols], ((0,), (0,)))
        return carry

    lax.fori_loop(0, chunks, state_step, 0)
    first[...] = total[...].astype(BF16)
    start("stage", 0)

    def advance(l):
        receive("stage", l)
        if l == 0:
            running[...] = total[mine] + buckets[0, mine].astype(F32)
        elif l + 1 < levels:
            running[...] = running[...] + buckets[l, mine].astype(F32)
        if l + 1 < levels:
            sends[l] = running[...].astype(BF16)
            start("stage", l + 1)
        if l > 0:
            start("pass", l)

    def column_arrived(j):
        receive("z", j)
        for kind in ("x", "y", "c0"):
            start(kind, j)

    def sides_arrived(j):
        receive("x", j)
        start("dy", j)
        receive("y", j)
        start("dx", j)
        start("c2", j)
        start("c4", j)

    def local_step(c, carry):
        load(q_hbm, q, 2, c).wait()
        at = pl.ds(pl.multiple_of(c * CHUNK, CHUNK), CHUNK)
        gate = gate_ref[at, :].astype(F32)
        causal = lax.broadcasted_iota(jnp.int32, (CHUNK, CHUNK), 0) >= lax.broadcasted_iota(
            jnp.int32, (CHUNK, CHUNK), 1
        )
        for h in range(heads):
            cols = slice(h * HEAD, (h + 1) * HEAD)
            query = q[at, cols]
            scores = dot(query, k[at, cols], ((1,), (1,)))
            scores = jnp.where(causal, scores, 0.0).astype(BF16)
            mixed = dot(scores, v[at, cols], ((1,), (0,))) + dot(query, prefix[c, h], ((1,), (0,)))
            acc[at, cols] = mixed * gate[:, h : h + 1]
        for step in range(chunks):
            @pl.when(c == step)
            def _():
                for l in range(levels - 1):
                    if min(l, chunks - 1) == step:
                        advance(l)
                for j in range(1, columns):
                    if min(j - 1, chunks - 1) == step:
                        column_arrived(j)
        return carry

    lax.fori_loop(0, chunks, local_step, 0)

    flags = [((me // (1 << l)) % 2).astype(F32) for l in range(levels)]

    for l in range(1, levels - 1):
        receive("pass", l)

    def early_step(c, carry):
        at = pl.ds(pl.multiple_of(c * CHUNK, CHUNK), CHUNK)
        gate = gate_ref[at, :].astype(F32)
        scaled = [gate[:, (l + 1) * heads : (l + 2) * heads] * flags[l] for l in range(levels - 1)]
        for h in range(heads):
            cols = slice(h * HEAD, (h + 1) * HEAD)
            query = q[at, cols]
            joined = jnp.concatenate([buckets[l, h] for l in range(levels - 1)], axis=1)
            product = dot(query, joined, ((1,), (0,)))
            sofar = acc[at, cols]
            for l in range(levels - 1):
                sofar = sofar + scaled[l][:, h : h + 1] * product[:, l * HEAD : (l + 1) * HEAD]
            acc[at, cols] = sofar
        for step in range(chunks):
            @pl.when(c == step)
            def _():
                for j in range(columns):
                    if min(j, chunks - 1) == step:
                        sides_arrived(j)
        return carry

    lax.fori_loop(0, chunks, early_step, 0)
    advance(levels - 1)
    receive("pass", levels - 1)

    def last_step(c, carry):
        at = pl.ds(pl.multiple_of(c * CHUNK, CHUNK), CHUNK)
        top = levels - 1
        scaled = gate_ref[at, (top + 1) * heads : (top + 2) * heads].astype(F32) * flags[top]
        for h in range(heads):
            cols = slice(h * HEAD, (h + 1) * HEAD)
            product = dot(q[at, cols], buckets[top, h], ((1,), (0,)))
            attended = acc[at, cols] + scaled[:, h : h + 1] * product
            squares = jnp.mean(attended * attended, axis=-1, keepdims=True)
            normed = attended * lax.rsqrt(squares + EPSILON) * gain_ref[:, cols]
            k[at, cols] = normed.astype(BF16)
        for step in range(chunks):
            @pl.when(c == step)
            def _():
                for j in range(columns):
                    if min(j, chunks - 1) == step:
                        receive("dy", j)
                        receive("dx", j)
                        start("c6", j)
        return carry

    lax.fori_loop(0, chunks, last_step, 0)
    own.wait()
    for kind in ("c0", "c2", "c4", "c6"):
        for j in range(columns):
            receive(kind, j)

    def store(c):
        at = pl.ds(pl.multiple_of(c * CHUNK, CHUNK), CHUNK)
        return pltpu.make_async_copy(v.at[at], out_hbm.at[at], load_sem.at[4, c])

    def project_step(c, carry):
        at = pl.ds(pl.multiple_of(c * CHUNK, CHUNK), CHUNK)
        v[at, :] = jnp.dot(k[at, :], whole[...], preferred_element_type=F32).astype(BF16)
        store(c).start()
        return carry

    lax.fori_loop(0, chunks, project_step, 0)
    for name in ids:
        send(name).wait_send()
    for c in range(chunks):
        store(c).wait()


def shards(queries, keys, values, level_gate, norm_gain, out_weight):
    n = lax.axis_size("ctx")
    rows, width = queries.shape
    heads, chunks = width // HEAD, rows // CHUNK
    levels = n.bit_length() - 1
    count = len(transfers(levels, n // 8))
    vmem = pl.BlockSpec(memory_space=pltpu.VMEM)
    hbm = pl.BlockSpec(memory_space=pl.ANY)
    return pl.pallas_call(
        functools.partial(kernel, n),
        out_shape=jax.ShapeDtypeStruct((rows, out_weight.shape[1]), BF16),
        in_specs=[hbm, hbm, hbm, vmem, vmem, vmem],
        out_specs=hbm,
        scratch_shapes=[
            pltpu.VMEM((rows, width), BF16),
            pltpu.VMEM((rows, width), BF16),
            pltpu.VMEM((rows, width), BF16),
            pltpu.VMEM((n * out_weight.shape[0], out_weight.shape[1]), BF16),
            pltpu.VMEM((rows, width), F32),
            pltpu.VMEM((chunks, heads, HEAD, HEAD), BF16),
            pltpu.VMEM((heads, HEAD, HEAD), F32),
            pltpu.VMEM((heads // 2, HEAD, HEAD), F32),
            pltpu.VMEM((levels, heads, HEAD, HEAD), BF16),
            pltpu.VMEM((heads, HEAD, HEAD), BF16),
            pltpu.VMEM((levels - 1, heads // 2, HEAD, HEAD), BF16),
            pltpu.SemaphoreType.DMA((5, chunks)),
            pltpu.SemaphoreType.DMA((count,)),
            pltpu.SemaphoreType.DMA((count,)),
        ],
        compiler_params=pltpu.CompilerParams(
            collective_id=0, has_side_effects=True, vmem_limit_bytes=60 * 1024 * 1024
        ),
        name="layer",
    )(queries, keys, values, level_gate, norm_gain.reshape(1, -1), out_weight)


def solution(mesh):
    placed = (P("ctx", None), P("ctx", None), P("ctx", None), P("ctx", None), P(), P("ctx", None))
    return jax.shard_map(
        shards, mesh=mesh, in_specs=placed, out_specs=P("ctx", None), check_vma=False
    )
```

time: 196 us -> 78.4 us (0.40)
  the two profiles are of different devices: /device:TPU:0 before, /device:TPU:9 now
where the time goes in v2:
time: 78.4 us; the launch traced here: 78.2 us
  Pallas kernels  73.4 us (94%)
  local copies, waits for them, and re-layouts  4.79 us (6%)
    pallas_call x1, Pallas kernels, shards(): pl.pallas_call(functools.partial(kernel, n), out_shape=jax.ShapeDtypeStru...  73.4 us
    unnamed x1, local copies, waits for them, and re-layouts  4.79 us

profile of v2, /device:TPU:9, one launch (start us, length us, event | category | flops | bytes accessed | tf_op | source)
XLA Modules:
  0.0 78.2 jit_solution(14196011236658724308)
XLA Ops:
  0.0 73.4 %layer.1 = bf16[1024,2048]{1,0:T(8,128)(2,1)} custom-call(bf16[1024,2048]{1,0:T(8,128)(2,1)} %q_hbm.1, bf16[1024,2048]{1,0:T(8,128)(2,1)} %k_hbm.1, bf16[1024,2048]{1,0:T(8,128)(2,1)} %v_hbm.1, bf16[1024,128]{1,0:T(8,128)(2,1)} %gate_ref.1, f32[1,2048]{1,0:T(1,128)} %bitcast.1, bf16[64,2048]{1,0:T(8,128)(2,1)} %w_ref.1), custom_call_target="tpu_custom_call" | custom-call | tf_op jit(solution)/shard_map/layer/pallas_call | solution.py:290
  73.4 4.8 %copy.8 = bf16[1024,2048]{1,0:T(8,128)(2,1)} copy(bf16[1024,2048]{1,0:T(8,128)(2,1)} %layer.1) | data formatting | bytes 8388608

commit v3 on v2

--- a/solution.py
+++ b/solution.py
@@ -29,15 +29,22 @@
 
 
 def transfers(levels, columns):
-    names = [("stage", l) for l in range(levels)] + [("pass", l) for l in range(1, levels)]
+    names = [("stage", 0)]
+    for l in range(1, levels):
+        names += [(kind, l, g) for kind in ("stage", "pass") for g in range(2)]
     names += [("z", j) for j in range(1, columns)]
     for kind in ("x", "y", "dx", "dy", "c0", "c2", "c4", "c6"):
         names += [(kind, j) for j in range(columns)]
     return {name: at for at, name in enumerate(names)}
 
 
-def kernel(n, q_hbm, k_hbm, v_hbm, gate_ref, gain_ref, w_ref, out_hbm,
-           q, k, v, whole, acc, prefix, total, running, buckets, first, sends, load_sem, send_sem, recv_sem):
+def plane_rows(me, column, part):
+    first_row = other(me, column << 3) // 8 * (8 * part)
+    return pl.ds(pl.multiple_of(first_row, 8 * part), 8 * part)
+
+
+def kernel(n, q_hbm, k_hbm, v_hbm, gate_ref, gain_ref, w_ref, acc, k, whole,
+           q, v, prefix, total, running, buckets, first, sends, load_sem, send_sem, recv_sem):
     rows, width = q.shape
     heads, chunks = width // HEAD, rows // CHUNK
     half = heads // 2
@@ -47,8 +54,11 @@
     ids = transfers(levels, columns)
     me = lax.axis_index("ctx")
     core = me % 2
-    mine = pl.ds(core * half, half)
-    yours = pl.ds((1 - core) * half, half)
+    group = half // 2
+
+    def part_of(core_bit, g):
+        return pl.ds(core_bit * half + g * group, group)
+
 
     def load(hbm, buffer, kind, c):
         at = pl.ds(c * CHUNK, CHUNK)
@@ -81,16 +91,20 @@
         return whole.at[at, pl.ds(side * width_here, width_here)]
 
     def send(name):
-        kind, j = name
-        if kind == "stage":
-            if j == 0:
-                return copy(name, first, buckets.at[0], 1)
-            return copy(name, sends.at[j - 1], buckets.at[j, mine], 1 << j)
-        if kind == "pass":
-            return copy(name, buckets.at[j, mine], buckets.at[j, mine], 1)
+        kind, j = name[:2]
+        if kind == "stage" and j == 0:
+            return copy(name, first, buckets.at[0], 1)
+        if kind in ("stage", "pass"):
+            here = buckets.at[j, part_of(core, name[2])]
+            if kind == "stage":
+                return copy(name, sends.at[j - 1, pl.ds(name[2] * group, group)], here, 1 << j)
+            return copy(name, here, here, 1)
         col = j << 3
         if kind == "z":
-            return copy(name, w_ref, shard(0), col)
+            low = j & -j
+            if low == j:
+                return copy(name, w_ref, shard(0), col)
+            return copy(name, shard((j ^ low) << 3), shard((j ^ low) << 3), low << 3)
         if kind in ("x", "y", "c0"):
             mask = {"x": 2, "y": 4, "c0": 1}[kind]
             return copy(name, w_ref if j == 0 else shard(col), shard(col), mask)
@@ -98,19 +112,21 @@
             return copy(name, shard(2 ^ col, 0), shard(2 ^ col, 0), 4)
         if kind == "dx":
             return copy(name, shard(4 ^ col, 1), shard(4 ^ col, 1), 2)
-        group = int(kind[1])
-        return copy(name, shard(group ^ col), shard(group ^ col), 1)
+        block = int(kind[1])
+        return copy(name, shard(block ^ col), shard(block ^ col), 1)
 
     def arrival(name):
-        kind, j = name
-        if kind == "stage":
-            dst, mask = (buckets.at[0], 1) if j == 0 else (buckets.at[j, mine], 1 << j)
+        kind, j = name[:2]
+        if kind == "stage" and j == 0:
+            dst, mask = buckets.at[0], 1
+        elif kind == "stage":
+            dst, mask = buckets.at[j, part_of(core, name[2])], 1 << j
         elif kind == "pass":
-            dst, mask = buckets.at[j, yours], 1
+            dst, mask = buckets.at[j, part_of(1 - core, name[2])], 1
         else:
             col = j << 3
             if kind == "z":
-                dst, mask = shard(col), col
+                dst, mask = shard(col), (j & -j) << 3
             elif kind in ("x", "y"):
                 mask = {"x": 2, "y": 4}[kind]
                 dst = shard(mask ^ col)
@@ -130,8 +146,8 @@
 
     own = pltpu.make_async_copy(w_ref, shard(0), load_sem.at[3, 0])
     own.start()
-    for j in range(1, columns):
-        start("z", j)
+    for l in range(3, levels):
+        start("z", 1 << (l - 3))
     start("x", 0)
     start("y", 0)
     start("c0", 0)
@@ -153,21 +169,33 @@
     first[...] = total[...].astype(BF16)
     start("stage", 0)
 
-    def advance(l):
-        receive("stage", l)
-        if l == 0:
-            running[...] = total[mine] + buckets[0, mine].astype(F32)
-        elif l + 1 < levels:
-            running[...] = running[...] + buckets[l, mine].astype(F32)
+    def send_on(l, g):
+        at = pl.ds(g * group, group)
+        sends[l, at] = running[at].astype(BF16)
+        start("stage", l + 1, g)
+
+    def advance(l, g):
+        receive("stage", l, g)
         if l + 1 < levels:
-            sends[l] = running[...].astype(BF16)
-            start("stage", l + 1)
-        if l > 0:
-            start("pass", l)
-
-    def column_arrived(j):
+            at = pl.ds(g * group, group)
+            running[at] = running[at] + buckets[l, part_of(core, g)].astype(F32)
+            send_on(l, g)
+        start("pass", l, g)
+
+    def advance_first():
+        receive("stage", 0)
+        at = pl.ds(core * half, half)
+        running[...] = total[at] + buckets[0, at].astype(F32)
+        for g in range(2):
+            send_on(0, g)
+
+    def column_arrived(j, kinds):
         receive("z", j)
-        for kind in ("x", "y", "c0"):
+        bit = 1
+        while bit < (j & -j):
+            start("z", j | bit)
+            bit *= 2
+        for kind in kinds:
             start(kind, j)
 
     def sides_arrived(j):
@@ -192,23 +220,47 @@
             scores = jnp.where(causal, scores, 0.0).astype(BF16)
             mixed = dot(scores, v[at, cols], ((1,), (0,))) + dot(query, prefix[c, h], ((1,), (0,)))
             acc[at, cols] = mixed * gate[:, h : h + 1]
-        for step in range(chunks):
-            @pl.when(c == step)
-            def _():
-                for l in range(levels - 1):
-                    if min(l, chunks - 1) == step:
-                        advance(l)
-                for j in range(1, columns):
-                    if min(j - 1, chunks - 1) == step:
-                        column_arrived(j)
+            between(c, h, local_tasks)
         return carry
 
+    def between(c, h, tasks):
+        if (h + 1) % half:
+            return
+        for point, task in tasks.items():
+            if point % 2 == h // half:
+                pl.when(c == point // 2)(task)
+
+    def task_after_first():
+        advance_first()
+        start("x", 1)
+
+    def task_last_local():
+        advance(1, 1)
+        start("x", 2)
+        start("y", 2)
+
+    local_tasks = {
+        0: task_after_first,
+        3: lambda: column_arrived(2, ("c0",)),
+        4: lambda: advance(1, 0),
+        7: task_last_local,
+    }
+    column_arrived(1, ("y", "c0"))
     lax.fori_loop(0, chunks, local_step, 0)
+    advance(2, 0)
+    for j in range(3, columns):
+        column_arrived(j, ("x", "y", "c0"))
+    advance(2, 1)
+    sides_arrived(0)
+    for l in range(3, levels - 1):
+        for g in range(2):
+            advance(l, g)
 
     flags = [((me // (1 << l)) % 2).astype(F32) for l in range(levels)]
 
     for l in range(1, levels - 1):
-        receive("pass", l)
+        for g in range(2):
+            receive("pass", l, g)
 
     def early_step(c, carry):
         at = pl.ds(pl.multiple_of(c * CHUNK, CHUNK), CHUNK)
@@ -223,17 +275,29 @@
             for l in range(levels - 1):
                 sofar = sofar + scaled[l][:, h : h + 1] * product[:, l * HEAD : (l + 1) * HEAD]
             acc[at, cols] = sofar
-        for step in range(chunks):
-            @pl.when(c == step)
-            def _():
-                for j in range(columns):
-                    if min(j, chunks - 1) == step:
-                        sides_arrived(j)
+            between(c, h, early_tasks)
         return carry
 
+    def diagonal_arrived(j):
+        receive("dy", j)
+        receive("dx", j)
+        start("c6", j)
+
+    def task_sides_rest():
+        for j in range(3, columns):
+            sides_arrived(j)
+
+    early_tasks = {
+        0: lambda: sides_arrived(1),
+        3: lambda: sides_arrived(2),
+        5: lambda: diagonal_arrived(0),
+        6: task_sides_rest,
+    }
     lax.fori_loop(0, chunks, early_step, 0)
-    advance(levels - 1)
-    receive("pass", levels - 1)
+    for g in range(2):
+        advance(levels - 1, g)
+    for g in range(2):
+        receive("pass", levels - 1, g)
 
     def last_step(c, carry):
         at = pl.ds(pl.multiple_of(c * CHUNK, CHUNK), CHUNK)
@@ -246,37 +310,43 @@
             squares = jnp.mean(attended * attended, axis=-1, keepdims=True)
             normed = attended * lax.rsqrt(squares + EPSILON) * gain_ref[:, cols]
             k[at, cols] = normed.astype(BF16)
-        for step in range(chunks):
-            @pl.when(c == step)
-            def _():
-                for j in range(columns):
-                    if min(j, chunks - 1) == step:
-                        receive("dy", j)
-                        receive("dx", j)
-                        start("c6", j)
+            between(c, h, last_tasks)
         return carry
 
+    last_tasks = {2: lambda: diagonal_arrived(1), 5: lambda: diagonal_arrived(2)}
     lax.fori_loop(0, chunks, last_step, 0)
     own.wait()
-    for kind in ("c0", "c2", "c4", "c6"):
-        for j in range(columns):
+
+    def column_ready(j):
+        for kind in ("c0", "c2", "c4", "c6"):
             receive(kind, j)
 
-    def store(c):
-        at = pl.ds(pl.multiple_of(c * CHUNK, CHUNK), CHUNK)
-        return pltpu.make_async_copy(v.at[at], out_hbm.at[at], load_sem.at[4, c])
-
-    def project_step(c, carry):
-        at = pl.ds(pl.multiple_of(c * CHUNK, CHUNK), CHUNK)
-        v[at, :] = jnp.dot(k[at, :], whole[...], preferred_element_type=F32).astype(BF16)
-        store(c).start()
-        return carry
-
-    lax.fori_loop(0, chunks, project_step, 0)
+    def project(j):
+        planes = plane_rows(me, j, part)
+
+        def project_step(c, carry):
+            at = pl.ds(pl.multiple_of(c * CHUNK, CHUNK), CHUNK)
+            product = jnp.dot(k[at, planes], whole[planes, :], preferred_element_type=F32)
+            acc[at, :] = product if j == 0 else acc[at, :] + product
+            return carry
+
+        lax.fori_loop(0, chunks, project_step, 0)
+
+    for j in range(columns - 1):
+        column_ready(j)
+        project(j)
+        if j + 3 < columns:
+            diagonal_arrived(j + 3)
+    column_ready(columns - 1)
     for name in ids:
         send(name).wait_send()
-    for c in range(chunks):
-        store(c).wait()
+
+
+def project_kernel(n, part, acc_ref, normed_ref, whole_ref, out_ref):
+    planes = plane_rows(lax.axis_index("ctx"), n // 8 - 1, part)
+    at = pl.ds(pl.multiple_of(pl.program_id(0) * CHUNK, CHUNK), CHUNK)
+    product = jnp.dot(normed_ref[at, planes], whole_ref[planes, :], preferred_element_type=F32)
+    out_ref[...] = (acc_ref[at, :] + product).astype(BF16)
 
 
 def shards(queries, keys, values, level_gate, norm_gain, out_weight):
@@ -286,18 +356,21 @@
     levels = n.bit_length() - 1
     count = len(transfers(levels, n // 8))
     vmem = pl.BlockSpec(memory_space=pltpu.VMEM)
-    hbm = pl.BlockSpec(memory_space=pl.ANY)
-    return pl.pallas_call(
+    hbm = pl.BlockSpec(memory_space=pltpu.HBM)
+    out_width = out_weight.shape[1]
+    weight_rows = n * out_weight.shape[0]
+    acc, normed, whole = pl.pallas_call(
         functools.partial(kernel, n),
-        out_shape=jax.ShapeDtypeStruct((rows, out_weight.shape[1]), BF16),
+        out_shape=[
+            pltpu.VMEM((rows, width), F32),
+            pltpu.VMEM((rows, width), BF16),
+            pltpu.VMEM((weight_rows, out_width), BF16),
+        ],
         in_specs=[hbm, hbm, hbm, vmem, vmem, vmem],
-        out_specs=hbm,
+        out_specs=[vmem] * 3,
         scratch_shapes=[
             pltpu.VMEM((rows, width), BF16),
             pltpu.VMEM((rows, width), BF16),
-            pltpu.VMEM((rows, width), BF16),
-            pltpu.VMEM((n * out_weight.shape[0], out_weight.shape[1]), BF16),
-            pltpu.VMEM((rows, width), F32),
             pltpu.VMEM((chunks, heads, HEAD, HEAD), BF16),
             pltpu.VMEM((heads, HEAD, HEAD), F32),
             pltpu.VMEM((heads // 2, HEAD, HEAD), F32),
@@ -309,10 +382,19 @@
             pltpu.SemaphoreType.DMA((count,)),
         ],
         compiler_params=pltpu.CompilerParams(
-            collective_id=0, has_side_effects=True, vmem_limit_bytes=60 * 1024 * 1024
+            collective_id=0, has_side_effects=True, vmem_limit_bytes=38 * 1024 * 1024
         ),
         name="layer",
     )(queries, keys, values, level_gate, norm_gain.reshape(1, -1), out_weight)
+    return pl.pallas_call(
+        functools.partial(project_kernel, n, out_weight.shape[0]),
+        grid=(chunks,),
+        out_shape=jax.ShapeDtypeStruct((rows, out_width), BF16),
+        in_specs=[vmem] * 3,
+        out_specs=pl.BlockSpec((CHUNK, out_width), lambda i: (i, 0)),
+        compiler_params=pltpu.CompilerParams(vmem_limit_bytes=12 * 1024 * 1024),
+        name="project",
+    )(acc, normed, whole)
 
 
 def solution(mesh):

time: 78.4 us -> 74.7 us (0.953)
  the two profiles are of different devices: /device:TPU:9 before, /device:TPU:0 now
where the time goes in v3:
time: 74.7 us; the launch traced here: 73.5 us
  Pallas kernels  73.5 us (98%)
    pallas_call x1, Pallas kernels, shards(): pl.pallas_call(functools.partial(kernel, n), out_shape=[pltpu.VMEM((rows,...  69.3 us
    pallas_call x1, Pallas kernels, shards(): pl.pallas_call(functools.partial(project_kernel, n, out_weight.shape[0]),...  4.2 us

profile of v3, /device:TPU:0, one launch (start us, length us, event | category | flops | bytes accessed | tf_op | source)
XLA Modules:
  0.0 73.5 jit_solution(10124993327897185373)
XLA Ops:
  0.0 69.3 %layer.1 = (f32[1024,2048]{1,0:T(8,128)S(1)}, bf16[1024,2048]{1,0:T(8,128)(2,1)S(1)}, bf16[2048,2048]{1,0:T(8,128)(2,1)S(1)}) custom-call(bf16[1024,2048]{1,0:T(8,128)(2,1)} %q_hbm.1, bf16[1024,2048]{1,0:T(8,128)(2,1)} %k_hbm.1, bf16[1024,2048]{1,0:T(8,128)(2,1)} %v_hbm.1, bf16[1024,128]{1,0:T(8,128)(2,1)} %gate_ref.1, f32[1,2048]{1,0:T(1,128)} %bitcast.1, ...), custom_call_target="tpu_custom_call" | custom-call | tf_op jit(solution)/shard_map/layer/pallas_call | solution.py:362
  69.3 4.2 %project.1 = bf16[1024,2048]{1,0:T(8,128)(2,1)} custom-call(f32[1024,2048]{1,0:T(8,128)S(1)} %get-tuple-element.8.acc_ref, bf16[1024,2048]{1,0:T(8,128)(2,1)S(1)} %get-tuple-element.9.normed_ref, bf16[2048,2048]{1,0:T(8,128)(2,1)S(1)} %get-tuple-element.10.whole_ref), custom_call_target="tpu_custom_call" | custom-call | tf_op jit(solution)/shard_map/project/pallas_call | solution.py:389
